TPU v7x, 256 devices: a whole 4x4x8 slice. The times are simulated.
256 devices in a mesh: row: 8 (over x, core), col: 32 (over y, z).
Axes of the slice: x: 4, y: 4, z: 8, core: 2. Of those that a mesh axis runs over, the one named last changes fastest.
Arguments:
- src_coords: int32 [3, 131072], P(None, 'row'), may hold values from 0 to 51
- tgt_coords: int32 [3, 262144], P(None, 'col'), may hold values from 0 to 51
- src_mass: int32 [131072], P('row'), may hold values from 1 to 298
- tgt_mass: int32 [262144], P('col'), may hold values from 1 to 298
- tgt_start: float32 [262144], P('col'), may hold values from -10 to 170
- kept_src: int32 [8, 32, 64], P('row', 'col'), may hold values from 0 to 127, as said below
- kept_tgt: int32 [8, 32, 64], P('row', 'col'), may hold values from 0 to 63, as said below
- kept_count: int32 [8, 32], P('row', 'col'), may hold values from 1 to 64, as said below
Outputs:
- src_potential: float32 [131072], P('row')
- tgt_potential: float32 [262144], P('col')
Inputs may be any that keep to these rules, and one draw needn't show every extreme that they name: `kept_src`: every source tile lies in a live pair of some device of its row block. Slots at or past a device's count hold pairs that are not live. `kept_tgt`: every target tile lies in a live pair of some device of its column block. `kept_count`: some device has exactly 64 live slots in every draw.
All inputs are finite; a program needn't handle non-finite values.
Results may differ from a plain program's by a relative error of at most 0.0001.
Values sent between devices are 32-bit elements; how exact they have to be, the bound alone decides.
No kernel may reach another device: no remote copies, remote signals or barrier semaphores. Data moves between devices by JAX's collectives and lax.ppermute only.
A program may use at most 64 MiB of HBM per device.

v0:
```python
import jax
import jax.numpy as jnp
from jax import lax
from jax.sharding import PartitionSpec as P

ITERS = 3


very_negative = -1e30
cost_scale = 0.05


def tile_costs(src_coords, tgt_coords, src_ids, tgt_ids):
    src_tiles = jnp.take(src_coords.reshape(3, -1, 128), src_ids, axis=1).astype(jnp.float32)
    tgt_tiles = jnp.take(tgt_coords.reshape(3, -1, 128), tgt_ids, axis=1).astype(jnp.float32)
    square = None
    for component in range(3):
        difference = src_tiles[component][:, :, None] - tgt_tiles[component][:, None, :]
        square = difference * difference if component == 0 else square + difference * difference
    return cost_scale * square


def slot_partials(scores, live_slots, reduce_dim):
    peak_values = jnp.max(scores, axis=reduce_dim)
    totals = jnp.sum(jnp.exp(scores - jnp.expand_dims(peak_values, reduce_dim)), axis=reduce_dim)
    return (
        jnp.where(live_slots[:, None], peak_values, very_negative),
        jnp.where(live_slots[:, None], totals, 0.0),
    )


def fold_tiles(peak_values, totals, tile_ids, tile_count):
    member = tile_ids[:, None] == jnp.arange(tile_count, dtype=jnp.int32)[None, :]
    tile_peak = jnp.max(
        jnp.where(member[:, :, None], peak_values[:, None, :], very_negative), axis=0
    )
    slot_peak = jnp.take(tile_peak, tile_ids, axis=0)
    weighted = totals * jnp.exp(peak_values - slot_peak)
    tile_total = jnp.dot(member.astype(jnp.float32).T, weighted, precision=lax.Precision.HIGHEST)
    return (tile_peak.reshape(-1), tile_total.reshape(-1))


def row_merge(tile_peak, tile_total, src_log):
    highest = lax.pmax(tile_peak, "col")
    summed = lax.psum(tile_total * jnp.exp(tile_peak - highest), "col")
    return src_log - (highest + jnp.log(summed))


def col_merge(tile_peak, tile_total, tgt_log):
    highest = lax.pmax(tile_peak, "row")
    summed = lax.psum(tile_total * jnp.exp(tile_peak - highest), "row")
    return tgt_log - (highest + jnp.log(summed))


def on_device(
    src_coords, tgt_coords, src_mass, tgt_mass, tgt_start, kept_src, kept_tgt, kept_count
):
    src_ids = kept_src[0, 0]
    tgt_ids = kept_tgt[0, 0]
    live_slots = jnp.arange(src_ids.shape[0], dtype=jnp.int32) < kept_count[0, 0]
    src_tiles_count = src_coords.shape[1] // 128
    tgt_tiles_count = tgt_coords.shape[1] // 128
    src_weight = src_mass.astype(jnp.float32)
    tgt_weight = tgt_mass.astype(jnp.float32)
    src_sum = lax.psum(jnp.sum(src_weight), "row")
    tgt_sum = lax.psum(jnp.sum(tgt_weight), "col")
    src_log = jnp.log(src_weight) - jnp.log(src_sum)
    tgt_log = jnp.log(tgt_weight) - jnp.log(tgt_sum)
    cost = tile_costs(src_coords, tgt_coords, src_ids, tgt_ids)
    tgt_potential = tgt_start
    src_potential = None
    for iteration in range(ITERS):
        tgt_picked = jnp.take(tgt_potential.reshape(-1, 128), tgt_ids, axis=0)
        peak_values, totals = slot_partials(tgt_picked[:, None, :] - cost, live_slots, 2)
        tile_peak, tile_total = fold_tiles(peak_values, totals, src_ids, src_tiles_count)
        src_potential = row_merge(tile_peak, tile_total, src_log)
        src_picked = jnp.take(src_potential.reshape(-1, 128), src_ids, axis=0)
        peak_values, totals = slot_partials(src_picked[:, :, None] - cost, live_slots, 1)
        tile_peak, tile_total = fold_tiles(peak_values, totals, tgt_ids, tgt_tiles_count)
        tgt_potential = col_merge(tile_peak, tile_total, tgt_log)
    return (src_potential, tgt_potential)


def solution(mesh):
    placed = (
        P(None, "row"),
        P(None, "col"),
        P("row"),
        P("col"),
        P("col"),
        P("row", "col", None),
        P("row", "col", None),
        P("row", "col"),
    )
    return jax.shard_map(
        on_device, mesh=mesh, in_specs=placed, out_specs=(P("row"), P("col")), check_vma=False
    )
```

profile of v0, /device:TPU:1, one launch (start us, length us, event | category | flops | bytes accessed | tf_op | source)
XLA Modules:
  0.0 1062.6 jit_solution(4097321126829979318)
XLA Ops:
  15.0 5.1 subtract_reduce_fusion.5
  20.2 2.0 select_reduce_fusion.2
  22.3 6.4 exponential_reduce_fusion.5
  30.8 130.7 %all-reduce.7.cloned.1.call-done = f32[16384]{0:T(1024)} async-done(((f32[16384]{0:T(1024)}), f32[16384]{0:T(1024)}) %all-reduce.7.cloned.1.call-update) | async-done | bytes 65552 | tf_op jit(solution)/shard_map/pmax | solution.py:44
  161.5 1.9 fusion
  163.5 59.3 %psum.57 = f32[]{:T(128)} all-reduce(f32[]{:T(128)} %convert_reduce_fusion.1), channel_id=1, replica_groups=mesh['row'=8,'col'=32] {'col'}, use_global_device_ids=true, to_apply=%region_3.0 | all-reduce | flops 1 | bytes 8 | tf_op jit(solution)/shard_map/psum | solution.py:66
  222.8 31.2 %psum.56 = f32[]{:T(128)} all-reduce(f32[]{:T(128)} %convert_reduce_fusion), channel_id=1, replica_groups=mesh['row'=8,'col'=32] {'row'}, use_global_device_ids=true, to_apply=%region_1.0 | all-reduce | flops 1 | bytes 8 | tf_op jit(solution)/shard_map/psum | solution.py:65
  255.4 47.9 %all-reduce.9.cloned.1.call-done = f32[16384]{0:T(1024)} async-done(((f32[16384]{0:T(1024)}), f32[16384]{0:T(1024)}) %all-reduce.9.cloned.1.call-update) | async-done | bytes 65552 | tf_op jit(solution)/shard_map/psum | solution.py:45
  304.8 5.0 subtract_reduce_fusion.4
  309.8 5.1 exponential_reduce_fusion.4
  316.2 24.8 %pmax.43 = f32[8192]{0:T(1024)S(1)} all-reduce(f32[8192]{0:T(1024)S(1)} %bitcast.78), channel_id=1, replica_groups=mesh['row'=8,'col'=32] {'row'}, use_global_device_ids=true, to_apply=%region_11.14 | all-reduce | flops 8192 | bytes 65536 | tf_op jit(solution)/shard_map/pmax | solution.py:50
  341.3 23.6 %psum.59 = f32[8192]{0:T(1024)S(1)} all-reduce(f32[8192]{0:T(1024)S(1)} %fusion.3), channel_id=1, replica_groups=mesh['row'=8,'col'=32] {'row'}, use_global_device_ids=true, to_apply=%region_13.16 | all-reduce | flops 8192 | bytes 65536 | tf_op jit(solution)/shard_map/psum | solution.py:51
  365.6 5.1 subtract_reduce_fusion.3
  370.8 2.0 select_reduce_fusion.1
  372.9 6.4 exponential_reduce_fusion.3
  379.9 127.0 %all-reduce.11.cloned.1.call-done = f32[16384]{0:T(1024)} async-done(((f32[16384]{0:T(1024)}), f32[16384]{0:T(1024)}) %all-reduce.11.cloned.1.call-update) | async-done | bytes 65552 | tf_op jit(solution)/shard_map/pmax | solution.py:44
  506.9 1.9 fusion.1
  508.8 139.3 %all-reduce.13.cloned.1.call-done = f32[16384]{0:T(1024)} async-done(((f32[16384]{0:T(1024)}), f32[16384]{0:T(1024)}) %all-reduce.13.cloned.1.call-update) | async-done | bytes 65552 | tf_op jit(solution)/shard_map/psum | solution.py:45
  649.6 5.0 subtract_reduce_fusion.2
  654.6 5.1 exponential_reduce_fusion.2
  661.1 24.8 %pmax.45 = f32[8192]{0:T(1024)S(1)} all-reduce(f32[8192]{0:T(1024)S(1)} %bitcast.79), channel_id=1, replica_groups=mesh['row'=8,'col'=32] {'row'}, use_global_device_ids=true, to_apply=%region_21.24 | all-reduce | flops 8192 | bytes 65536 | tf_op jit(solution)/shard_map/pmax | solution.py:50
  686.1 23.6 %psum.61 = f32[8192]{0:T(1024)S(1)} all-reduce(f32[8192]{0:T(1024)S(1)} %fusion.4), channel_id=1, replica_groups=mesh['row'=8,'col'=32] {'row'}, use_global_device_ids=true, to_apply=%region_23.26 | all-reduce | flops 8192 | bytes 65536 | tf_op jit(solution)/shard_map/psum | solution.py:51
  710.4 5.1 subtract_reduce_fusion.1
  715.6 2.0 select_reduce_fusion
  717.9 6.4 exponential_reduce_fusion.1
  725.0 126.9 %all-reduce.15.cloned.1.call-done = f32[16384]{0:T(1024)} async-done(((f32[16384]{0:T(1024)}), f32[16384]{0:T(1024)}) %all-reduce.15.cloned.1.call-update) | async-done | bytes 65552 | tf_op jit(solution)/shard_map/pmax | solution.py:44
  851.9 1.9 fusion.2
  853.7 139.7 %all-reduce.17.cloned.1.call-done = f32[16384]{0:T(1024)} async-done(((f32[16384]{0:T(1024)}), f32[16384]{0:T(1024)}) %all-reduce.17.cloned.1.call-update) | async-done | bytes 65552 | tf_op jit(solution)/shard_map/psum | solution.py:45
  995.0 5.0 subtract_reduce_fusion
  1000.0 5.1 exponential_reduce_fusion
  1006.5 24.8 %pmax.47 = f32[8192]{0:T(1024)S(1)} all-reduce(f32[8192]{0:T(1024)S(1)} %bitcast.77), channel_id=1, replica_groups=mesh['row'=8,'col'=32] {'row'}, use_global_device_ids=true, to_apply=%region_31.34 | all-reduce | flops 8192 | bytes 65536 | tf_op jit(solution)/shard_map/pmax | solution.py:50
  1031.5 23.6 %psum.63 = f32[8192]{0:T(1024)S(1)} all-reduce(f32[8192]{0:T(1024)S(1)} %fusion.5), channel_id=1, replica_groups=mesh['row'=8,'col'=32] {'row'}, use_global_device_ids=true, to_apply=%region_33.36 | all-reduce | flops 8192 | bytes 65536 | tf_op jit(solution)/shard_map/psum | solution.py:51
  (96 shorter events, 22.7 us)
Async XLA Ops:
  7.2 4.1 copy-start
  7.2 154.3 %all-reduce.7.cloned.1.call-start = ((), (), s32[]{:S(2)}) async-start(), calls=%async_computation | async-start | bytes 131072 | tf_op jit(solution)/shard_map/pmax | solution.py:44
  11.9 0.9 copy-start.11
  13.5 0.8 copy-start.4
  13.6 1.3 copy-start.12
  22.2 6.5 copy-start.1
  22.3 281.0 %all-reduce.9.cloned.1.call-start = ((), (), s32[]{:S(2)}) async-start(), calls=%async_computation.1 | async-start | bytes 131072 | tf_op jit(solution)/shard_map/psum | solution.py:45
  28.7 0.8 copy-start.6
  28.7 1.4 copy-start.7
  29.6 133.8 %copy-start.13 = (s32[1,1,64]{2,1,0:T(1,128)S(1)}, s32[1,1,64]{2,1,0:T(1,128)}, u32[]{:S(2)}) copy-start(s32[1,1,64]{2,1,0:T(1,128)} %param.18) | copy-start | bytes 772
  161.5 141.8 %copy-start.8 = (f32[16384]{0:T(1024)S(1)}, f32[16384]{0:T(1024)}, u32[]{:S(2)}) copy-start(f32[16384]{0:T(1024)} %all-reduce.7.cloned.1.call-done) | copy-start | bytes 196612
  163.4 343.5 %all-reduce.11.cloned.1.call-start = ((), (), s32[]{:S(2)}) async-start(), calls=%async_computation.2 | async-start | bytes 131072 | tf_op jit(solution)/shard_map/pmax | solution.py:44
  372.8 6.5 copy-start.3
  372.9 275.2 %all-reduce.13.cloned.1.call-start = ((), (), s32[]{:S(2)}) async-start(), calls=%async_computation.3 | async-start | bytes 131072 | tf_op jit(solution)/shard_map/psum | solution.py:45
  506.9 141.2 %copy-start.9 = (f32[16384]{0:T(1024)S(1)}, f32[16384]{0:T(1024)}, u32[]{:S(2)}) copy-start(f32[16384]{0:T(1024)} %all-reduce.11.cloned.1.call-done) | copy-start | bytes 196612
  508.8 343.1 %all-reduce.15.cloned.1.call-start = ((), (), s32[]{:S(2)}) async-start(), calls=%async_computation.4 | async-start | bytes 131072 | tf_op jit(solution)/shard_map/pmax | solution.py:44
  717.7 6.7 copy-start.2
  717.7 275.8 %all-reduce.17.cloned.1.call-start = ((), (), s32[]{:S(2)}) async-start(), calls=%async_computation.5 | async-start | bytes 131072 | tf_op jit(solution)/shard_map/psum | solution.py:45
  851.8 141.6 %copy-start.10 = (f32[16384]{0:T(1024)S(1)}, f32[16384]{0:T(1024)}, u32[]{:S(2)}) copy-start(f32[16384]{0:T(1024)} %all-reduce.15.cloned.1.call-done) | copy-start | bytes 196612
  994.3 5.7 copy-start.5
Sparse Core Ops, SparseCore 0:
  22.4 139.0 all-reduce.6
  165.9 137.2 all-reduce.8
  373.0 133.8 all-reduce.10
  510.8 137.2 all-reduce.12
  717.8 133.9 all-reduce.14
  856.1 137.2 all-reduce.16
where the time goes:
time: 1070 us; the launch traced here: 1060 us
  waiting for transfers between devices  711 us (66%)
  blocking collectives  236 us (22%)
  other arithmetic  82.2 us (8%)
  between operations  16.4 us (2%)
    pmax x3, waiting for transfers between devices, row_merge(): highest = lax.pmax(tile_peak, 'col')  385 us
    psum x3, waiting for transfers between devices, row_merge(): summed = lax.psum(tile_total * jnp.exp(tile_peak - highest), 'col')  327 us
    pmax x3, blocking collectives, col_merge(): highest = lax.pmax(tile_peak, 'row')  74.3 us
    psum x3, blocking collectives, col_merge(): summed = lax.psum(tile_total * jnp.exp(tile_peak - highest), 'row')  70.8 us
    psum x1, blocking collectives, on_device(): tgt_sum = lax.psum(jnp.sum(tgt_weight), 'col')  59.3 us
    reduce_sum x6, other arithmetic, slot_partials(): jnp.sum(jnp.exp(scores - jnp.expand_dims(peak_values, reduce_dim)), axis=...  34.4 us
    psum x1, blocking collectives, on_device(): src_sum = lax.psum(jnp.sum(src_weight), 'row')  31.2 us
    reduce_max x6, other arithmetic, slot_partials(): peak_values = jnp.max(scores, axis=reduce_dim)  30.4 us
  transfers between devices with their start and end apart: 6, of which 6 were waited for; matrix products, arithmetic and copies ran while one was open for 2% of the time, Pallas kernels for 0%

commit v1 on v0

v1 whole, which is shorter than its diff:
```python
import functools

import jax
import jax.numpy as jnp
from jax import lax
from jax.experimental import pallas as pl
from jax.experimental.pallas import tpu as pltpu
from jax.sharding import PartitionSpec as P

ITERS = 3
NONE = -1.0e30
UNITS = 20.0
STEP = 0.05
GROUP = 8


def lse(parts):
    top = functools.reduce(jnp.maximum, parts)
    terms = [jnp.exp(p - top) for p in parts]
    while len(terms) > 1:
        half = len(terms) // 2
        terms = [terms[k] + terms[k + half] for k in range(half)]
    return top + jnp.log(terms[0])


def features(coords):
    tiles = coords.reshape(3, -1, 1, 128)
    x, y, z = tiles[0], tiles[1], tiles[2]
    norm = x * x + y * y + z * z
    low = norm & 31
    high = norm - low
    one = jnp.ones_like(x)
    row = lax.broadcasted_iota(jnp.int32, (1, 16, 1), 1)

    def form(values):
        out = jnp.zeros((x.shape[0], 16, 128), jnp.int32)
        for index, value in enumerate(values):
            out = jnp.where(row == index, value, out)
        return out.astype(jnp.float32).astype(jnp.bfloat16)

    left = form([x, y, z, high, low, one, one])
    right = form([-2 * x, -2 * y, -2 * z, one, one, high, low])
    left = left.reshape(-1, 128, 128).transpose(0, 2, 1)
    return left, right


def half_step(potential, lane_ids_ref, sub_ids_ref, count_ref, left_ref, right_ref, peaks_ref, totals_ref, tops_ref, sums_ref, out_ref):
    sub_tiles = potential.shape[0]
    lane_tiles = tops_ref.shape[0]
    scaled = potential * UNITS
    if sub_tiles < 128:
        scaled = jnp.concatenate([scaled, jnp.zeros((128 - sub_tiles, 128), jnp.float32)], axis=0)
    columns = scaled.T
    count = count_ref[0, 0]
    peaks_ref[...] = jnp.full(peaks_ref.shape, NONE, jnp.float32)
    totals_ref[...] = jnp.ones(totals_ref.shape, jnp.float32)

    def group(g, carry):
        peaks, totals = [], []
        for u in range(GROUP):
            k = g * GROUP + u
            sub = sub_ids_ref[0, 0, k] & (sub_tiles - 1)
            lane = lane_ids_ref[0, 0, k] & (lane_tiles - 1)
            left = left_ref[sub >> 3]
            block = right_ref[lane]
            member = sub & 7
            right = jnp.concatenate(
                [jnp.where(member == q, block, jnp.zeros_like(block)) for q in range(8)], axis=0
            )
            square = jnp.dot(left, right, preferred_element_type=jnp.float32)
            value = jnp.take_along_axis(columns, jnp.full((128, 128), sub, jnp.int32), axis=1)
            score = value - square
            peak = jnp.max(score, axis=0, keepdims=True)
            total = jnp.sum(jnp.exp((score - peak) * STEP), axis=0, keepdims=True)
            peaks.append(jnp.where(k < count, peak * STEP, NONE))
            totals.append(total)
        start = pl.multiple_of(g * GROUP, GROUP)
        peaks_ref[pl.ds(start, GROUP), :] = jnp.concatenate(peaks, axis=0)
        totals_ref[pl.ds(start, GROUP), :] = jnp.concatenate(totals, axis=0)
        return carry

    lax.fori_loop(0, (count + (GROUP - 1)) // GROUP, group, 0)
    peaks_ref[...] = peaks_ref[...] + jnp.log(totals_ref[...])
    tops_ref[...] = jnp.full(tops_ref.shape, NONE, jnp.float32)
    sums_ref[...] = jnp.zeros(sums_ref.shape, jnp.float32)
    ids = [lane_ids_ref[0, 0, k] & (lane_tiles - 1) for k in range(64)]
    for k in range(64):
        at = pl.ds(ids[k], 1)
        tops_ref[at, :] = jnp.maximum(tops_ref[at, :], peaks_ref[k : k + 1, :])
    for k in range(64):
        totals_ref[k : k + 1, :] = jnp.exp(peaks_ref[k : k + 1, :] - tops_ref[pl.ds(ids[k], 1), :])
    for k in range(64):
        at = pl.ds(ids[k], 1)
        sums_ref[at, :] = sums_ref[at, :] + totals_ref[k : k + 1, :]
    sums = sums_ref[...]
    tops = tops_ref[...]
    out_ref[0:lane_tiles, :] = jnp.where(tops > 0.5 * NONE, tops + jnp.log(sums), NONE)


def put_total(out_ref, mass):
    rows = out_ref.shape[0]
    total = jnp.sum(jnp.sum(mass.astype(jnp.float32), axis=0, keepdims=True), axis=1, keepdims=True)
    out_ref[rows - 8 : rows, :] = jnp.broadcast_to(jnp.log(total), (8, 128))


def first_kernel(src_ids, tgt_ids, count, start, tgt_mass, left, right, out, peaks, totals, tops, sums):
    half_step(start[...], src_ids, tgt_ids, count, left, right, peaks, totals, tops, sums, out)
    put_total(out, tgt_mass[...])


def src_kernel(is_first, src_ids, tgt_ids, count, msg, src_mass, src_const, left, right, out, pot_ref, const_ref, peaks, totals, tops, sums):
    merged = lse([msg[k] for k in range(msg.shape[0])])
    const_ref[...] = merged[128:136]
    potential = jnp.log(src_mass[...].astype(jnp.float32)) - merged[0:128]
    if not is_first:
        potential = potential - src_const[0:1]
    pot_ref[...] = potential
    half_step(potential, tgt_ids, src_ids, count, left, right, peaks, totals, tops, sums, out)
    put_total(out, src_mass[...])


def tgt_value(is_first, parts, tgt_mass, tgt_const):
    merged = lse(parts)
    const = merged[64:72]
    potential = jnp.log(tgt_mass.astype(jnp.float32)) - tgt_const[0:1] - merged[0:64]
    if is_first:
        potential = potential + const[0:1]
    return potential, const


def tgt_kernel(is_first, src_ids, tgt_ids, count, m0, m1, m2, m3, tgt_mass, tgt_const, left, right, out, const_ref, peaks, totals, tops, sums):
    potential, const = tgt_value(is_first, [m0[...], m1[...], m2[...], m3[...]], tgt_mass[...], tgt_const[...])
    const_ref[...] = const
    half_step(potential, src_ids, tgt_ids, count, left, right, peaks, totals, tops, sums, out)
    put_total(out, tgt_mass[...])


SMEM = pl.BlockSpec(memory_space=pltpu.SMEM)
VMEM = pl.BlockSpec(memory_space=pltpu.VMEM)


def call(body, lane_tiles, extra_outs, *args):
    shape = jax.ShapeDtypeStruct
    return pl.pallas_call(
        body,
        out_shape=[shape((lane_tiles + 8, 128), jnp.float32)] + [shape(s, jnp.float32) for s in extra_outs],
        in_specs=[SMEM] * 3 + [VMEM] * (len(args) - 3),
        out_specs=[VMEM] * (1 + len(extra_outs)),
        scratch_shapes=[pltpu.VMEM((64, 128), jnp.float32)] * 2 + [pltpu.VMEM((lane_tiles, 128), jnp.float32)] * 2,
    )(*args)


def col_permute(value, shift):
    return lax.ppermute(value, "col", [(i, (i // 8 + shift) % 4 * 8 + i % 8) for i in range(32)])


def row_permute(value, shift):
    return lax.ppermute(value, "row", [(i, (i + 2 * shift) % 8) for i in range(8)])


Z_GROUPS = [[y * 8 + z for z in range(8)] for y in range(4)]


def over_col(message):
    merged = lse([message] + [col_permute(message, k) for k in (1, 2, 3)])
    copies = jnp.broadcast_to(merged[None], (8,) + merged.shape)
    return lax.all_to_all(copies, "col", 0, 0, tiled=True, axis_index_groups=Z_GROUPS)


def over_row(message):
    other = lax.ppermute(message, "row", [(i, i ^ 1) for i in range(8)])
    merged = lse([message, other])
    return [merged] + [row_permute(merged, k) for k in (1, 2, 3)]


def on_device(src_coords, tgt_coords, src_mass, tgt_mass, tgt_start, kept_src, kept_tgt, kept_count):
    src_mass = src_mass.reshape(128, 128)
    tgt_mass = tgt_mass.reshape(64, 128)
    src_left, src_right = features(src_coords)
    tgt_left, tgt_right = features(tgt_coords)
    lists = (kept_src, kept_tgt, kept_count)
    (message,) = call(first_kernel, 128, [], *lists, tgt_start.reshape(64, 128), tgt_mass, tgt_left, src_right)
    src_const = jnp.zeros((8, 128), jnp.float32)
    src_potential = None
    for iteration in range(ITERS):
        first = iteration == 0
        messages = over_col(message)
        message, src_potential, tgt_const = call(
            functools.partial(src_kernel, first), 64, [(128, 128), (8, 128)],
            *lists, messages, src_mass, src_const, src_left, tgt_right,
        )
        parts = over_row(message)
        if iteration + 1 < ITERS:
            message, src_const = call(
                functools.partial(tgt_kernel, first), 128, [(8, 128)],
                *lists, *parts, tgt_mass, tgt_const, tgt_left, src_right,
            )
    tgt_potential, _ = tgt_value(False, parts, tgt_mass, tgt_const)
    return src_potential.reshape(-1), tgt_potential.reshape(-1)


def solution(mesh):
    placed = (
        P(None, "row"),
        P(None, "col"),
        P("row"),
        P("col"),
        P("col"),
        P("row", "col", None),
        P("row", "col", None),
        P("row", "col"),
    )
    return jax.shard_map(
        on_device, mesh=mesh, in_specs=placed, out_specs=(P("row"), P("col")), check_vma=False
    )
```

time: 1070 us -> 164 us (0.15)
  waiting for transfers between devices: 711 us -> 35.6 us
  blocking collectives: 236 us -> 33.7 us
  other arithmetic: 82.2 us -> 12.9 us
  Pallas kernels: 0 us -> 32 us
  starting transfers between devices: 0.43 us -> 32.2 us
  between operations: 16.4 us -> 1.78 us
    pmax x3 -> x0, waiting for transfers between devices: 385 us -> none  [row_merge(): highest = lax.pmax(tile_peak, 'col')]
    psum x3 -> x0, waiting for transfers between devices: 327 us -> none  [row_merge(): summed = lax.psum(tile_total * jnp.exp(tile_peak - highest), 'col')]
    psum x5 -> x0, blocking collectives: 161 us -> none  [the longest x3 70.8 us: col_merge(): summed = lax.psum(tile_total * jnp.exp(tile_peak - highest), 'row')]
    pmax x3 -> x0, blocking collectives: 74.3 us -> none  [col_merge(): highest = lax.pmax(tile_peak, 'row')]
    reduce_max x12 -> x0, other arithmetic: 38.6 us -> none  [the longest x6 30.4 us: slot_partials(): peak_values = jnp.max(scores, axis=reduce_dim)]
    reduce_sum x8 -> x0, other arithmetic: 35.7 us -> none  [the longest x6 34.4 us: slot_partials(): jnp.sum(jnp.exp(scores - jnp.expand_dims(peak_values, reduce_dim)), axis=...]
    all_to_all x0 -> x2, blocking collectives: none -> 33.7 us  [over_col(): lax.all_to_all(copies, 'col', 0, 0, tiled=True, axis_index_groups=Z_GROUPS)]
    pallas_call x0 -> x6, Pallas kernels: none -> 32 us  [call(): pl.pallas_call(body, out_shape=[shape((lane_tiles + 8, 128), jnp.float32)...]
  transfers between devices with their start and end apart: 6 -> 22, of which waited for: 6 -> 20; matrix products, arithmetic and copies ran while one was open for 2% -> 6% of each run, Pallas kernels for 0% -> 0%
where the time goes in v1:
time: 164 us; the launch traced here: 162 us
  waiting for transfers between devices  35.6 us (22%)
  blocking collectives  33.7 us (21%)
  starting transfers between devices  32.2 us (20%)
  Pallas kernels  32 us (20%)
  local copies, waits for them, and re-layouts  14.1 us (9%)
  other arithmetic  12.9 us (8%)
  between operations  1.78 us (1%)
    all_to_all x2, blocking collectives, over_col(): lax.all_to_all(copies, 'col', 0, 0, tiled=True, axis_index_groups=Z_GROUPS)  33.7 us
    pallas_call x6, Pallas kernels, call(): pl.pallas_call(body, out_shape=[shape((lane_tiles + 8, 128), jnp.float32)...  32 us
    ppermute x9, waiting for transfers between devices, col_permute(): lax.ppermute(value, 'col', [(i, (i // 8 + shift) % 4 * 8 + i % 8) for i i...  15.3 us
    ppermute x9, starting transfers between devices, row_permute(): lax.ppermute(value, 'row', [(i, (i + 2 * shift) % 8) for i in range(8)])  9.31 us
    all_to_all x1, waiting for transfers between devices, over_col(): lax.all_to_all(copies, 'col', 0, 0, tiled=True, axis_index_groups=Z_GROUPS)  8.77 us
    ppermute x9, starting transfers between devices, col_permute(): lax.ppermute(value, 'col', [(i, (i // 8 + shift) % 4 * 8 + i % 8) for i i...  8.61 us
    ppermute x9, waiting for transfers between devices, row_permute(): lax.ppermute(value, 'row', [(i, (i + 2 * shift) % 8) for i in range(8)])  7.9 us
    all_to_all x1, starting transfers between devices, over_col(): lax.all_to_all(copies, 'col', 0, 0, tiled=True, axis_index_groups=Z_GROUPS)  7.61 us
  transfers between devices with their start and end apart: 22, of which 20 were waited for; matrix products, arithmetic and copies ran while one was open for 6% of the time, Pallas kernels for 0%

profile of v1, /device:TPU:1, one launch (start us, length us, event | category | flops | bytes accessed | tf_op | source)
XLA Modules:
  0.0 162.2 jit_solution(2770564616657300005)
XLA Ops:
  5.1 1.4 fusion.18
  7.2 1.2 convert_convert_fusion.1.right
  9.4 5.1 %shard_map.95 = f32[136,128]{1,0:T(8,128)} custom-call(s32[1,1,64]{2,1,0:T(1,128)} %src_ids.11, s32[1,1,64]{2,1,0:T(1,128)} %tgt_ids.11, s32[1,1]{1,0:T(1,128)S(6)} %copy.22.count, f32[64,128]{1,0:T(8,128)} %bitcast.57, s32[64,128]{1,0:T(8,128)} %bitcast.48, bf16[8,128,128]{2,1,0:T(8,128)(2,1)} %fusion.1.left, bf16[128,16,128]{2,1,0:T(8,128)(2,1)} %convert_convert_fusion.1.right), custom_call_target="tpu_custom_call" | custom-call | tf_op jit(solution)/shard_map/pallas_call | solution.py:144
  14.5 3.2 %collective-permute-start.2 = (f32[136,128]{1,0:T(8,128)}, f32[136,128]{1,0:T(8,128)S(1)}, u32[]{:S(2)}, u32[]{:S(2)}) collective-permute-start(f32[136,128]{1,0:T(8,128)} %shard_map.95), channel_id=1, source_target_pairs={{0,24},{1,25},{2,26},{3,27},{4,28},{5,29},{6,30},{7,31},{8,0},{9,1... | collective-permute-start | bytes 208904 | tf_op jit(solution)/shard_map/ppermute | solution.py:154
  19.8 5.0 %collective-permute-done = f32[136,128]{1,0:T(8,128)S(1)} collective-permute-done((f32[136,128]{1,0:T(8,128)}, f32[136,128]{1,0:T(8,128)S(1)}, u32[]{:S(2)}, u32[]{:S(2)}) %collective-permute-start) | collective-permute-done | bytes 69664 | tf_op jit(solution)/shard_map/ppermute | solution.py:154
  26.6 7.6 %all-to-all-start = ((f32[8,136,128]{2,1,0:T(8,128)}), f32[8,136,128]{2,1,0:T(8,128)}, u32[]{:S(2)}, u32[]{:S(2)}) async-start(f32[8,136,128]{2,1,0:T(8,128)} %broadcast_in_dim.420), calls=%async_computation | async-start | bytes 1114112 | tf_op jit(solution)/shard_map/all_to_all | solution.py:167
  35.1 1.4 copy.19
  36.5 1.3 copy.18
  38.0 1.3 copy.17
  41.0 3.2 %fusion.left = bf16[16,128,128]{2,1,0:T(8,128)(2,1)} fusion(s32[16,128,128]{1,2,0:T(8,128)S(1)} %copy.21, s32[16,128,128]{1,2,0:T(8,128)S(1)} %copy.20, s32[16,128,128]{1,2,0:T(8,128)} %copy.19, s32[16,128,128]{1,2,0:T(8,128)} %copy.18, s32[16,128,128]{1,2,0:T(8,128)} %copy.17, pred[128]{0:T(512)(128)(4,1)S(1)} %copy-done.20, ...), kind=kLoop, calls=%fused_computation.2 | loop fusion | flops 2359296 | bytes 5768064 | tf_op jit(solution)/shard_map/transpose | solution.py:43
  44.2 8.8 %all-to-all-done.msg = f32[8,136,128]{2,1,0:T(8,128)} async-done(((f32[8,136,128]{2,1,0:T(8,128)}), f32[8,136,128]{2,1,0:T(8,128)}, u32[]{:S(2)}, u32[]{:S(2)}) %all-to-all-start) | async-done | bytes 557088 | tf_op jit(solution)/shard_map/all_to_all | solution.py:167
  53.5 5.4 %shard_map.96 = (f32[72,128]{1,0:T(8,128)}, f32[128,128]{1,0:T(8,128)}, f32[8,128]{1,0:T(8,128)}) custom-call(s32[1,1,64]{2,1,0:T(1,128)} %src_ids.11, s32[1,1,64]{2,1,0:T(1,128)} %tgt_ids.11, s32[1,1]{1,0:T(1,128)S(6)} %copy.22.count, f32[8,136,128]{2,1,0:T(8,128)} %all-to-all-done.msg, s32[128,128]{1,0:T(8,128)} %bitcast.39, ...), custom_call_target="tpu_custom_call" | custom-call | tf_op jit(solution)/shard_map/pallas_call | solution.py:144
  58.9 1.4 collective-permute-done.3
  62.3 1.6 %collective-permute-start.6 = (f32[72,128]{1,0:T(8,128)S(1)}, f32[72,128]{1,0:T(8,128)S(1)}, u32[]{:S(2)}, u32[]{:S(2)}) collective-permute-start(f32[72,128]{1,0:T(8,128)S(1)} %log_add_fusion.5.m0), channel_id=1, source_target_pairs={{0,192},{32,224},{64,0},{96,32},{128,64},{160,96},{192,128},{224,1... | collective-permute-start | bytes 110600 | tf_op jit(solution)/shard_map/ppermute | solution.py:158
  63.9 1.3 collective-permute-done.4.m1
  67.2 5.4 %shard_map.97 = (f32[136,128]{1,0:T(8,128)}, f32[8,128]{1,0:T(8,128)}) custom-call(s32[1,1,64]{2,1,0:T(1,128)} %src_ids.11, s32[1,1,64]{2,1,0:T(1,128)} %tgt_ids.11, s32[1,1]{1,0:T(1,128)S(6)} %copy.22.count, f32[72,128]{1,0:T(8,128)} %copy-done.2, f32[72,128]{1,0:T(8,128)} %copy-done.5, f32[72,128]{1,0:T(8,128)} %copy-done.7, f32[72,128]{1,0:T(8,128)} %copy-done.9, ...), custom_call_target="tpu_custom_call" | custom-call | tf_op jit(solution)/shard_map/pallas_call | solution.py:144
  74.6 2.1 %collective-permute-done.9 = f32[136,128]{1,0:T(8,128)S(1)} collective-permute-done((f32[136,128]{1,0:T(8,128)}, f32[136,128]{1,0:T(8,128)S(1)}, u32[]{:S(2)}, u32[]{:S(2)}) %collective-permute-start.9) | collective-permute-done | bytes 69664 | tf_op jit(solution)/shard_map/ppermute | solution.py:154
  76.7 1.2 collective-permute-done.7
  77.9 1.2 collective-permute-done.8
  80.1 17.0 %all_to_all.15.msg = f32[8,136,128]{2,1,0:T(8,128)} all-to-all(f32[8,136,128]{2,1,0:T(8,128)S(1)} %broadcast_in_dim.449), channel_id=1, replica_groups={{0,1,2,3,4,5,6,7},{8,9,10,11,12,13,14,15},{16,17,18,19,20,21,22,23},{24..., dimensions={0} | all-to-all | bytes 1114112 | tf_op jit(solution)/shard_map/all_to_all | solution.py:167
  97.2 5.4 %shard_map.98 = (f32[72,128]{1,0:T(8,128)}, f32[128,128]{1,0:T(8,128)}, f32[8,128]{1,0:T(8,128)}) custom-call(s32[1,1,64]{2,1,0:T(1,128)} %src_ids.11, s32[1,1,64]{2,1,0:T(1,128)} %tgt_ids.11, s32[1,1]{1,0:T(1,128)S(6)} %copy.22.count, f32[8,136,128]{2,1,0:T(8,128)} %all_to_all.15.msg, s32[128,128]{1,0:T(8,128)} %bitcast.40, ...), custom_call_target="tpu_custom_call" | custom-call | tf_op jit(solution)/shard_map/pallas_call | solution.py:144
  102.6 3.2 %collective-permute-start.10 = (f32[72,128]{1,0:T(8,128)}, f32[72,128]{1,0:T(8,128)S(1)}, u32[]{:S(2)}, u32[]{:S(2)}) collective-permute-start(f32[72,128]{1,0:T(8,128)} %get-tuple-element.17), channel_id=1, source_target_pairs={{0,32},{32,0},{64,96},{96,64},{128,160},{160,128},{192,224},{224,1... | collective-permute-start | bytes 110600 | tf_op jit(solution)/shard_map/ppermute | solution.py:171
  107.7 3.7 %collective-permute-start.12 = (f32[72,128]{1,0:T(8,128)S(1)}, f32[72,128]{1,0:T(8,128)S(1)}, u32[]{:S(2)}, u32[]{:S(2)}) collective-permute-start(f32[72,128]{1,0:T(8,128)S(1)} %log_add_fusion.4.m0), channel_id=1, source_target_pairs={{0,128},{32,160},{64,192},{96,224},{128,0},{160,32},{192,64},{224,... | collective-permute-start | bytes 110600 | tf_op jit(solution)/shard_map/ppermute | solution.py:158
  111.7 1.4 collective-permute-done.12.m2
  114.8 5.2 %shard_map.99 = (f32[136,128]{1,0:T(8,128)}, f32[8,128]{1,0:T(8,128)}) custom-call(s32[1,1,64]{2,1,0:T(1,128)} %src_ids.11, s32[1,1,64]{2,1,0:T(1,128)} %tgt_ids.11, s32[1,1]{1,0:T(1,128)S(6)} %copy.22.count, f32[72,128]{1,0:T(8,128)} %copy-done.1, f32[72,128]{1,0:T(8,128)} %copy-done.4, f32[72,128]{1,0:T(8,128)} %copy-done.6, f32[72,128]{1,0:T(8,128)} %copy-done.8, ...), custom_call_target="tpu_custom_call" | custom-call | tf_op jit(solution)/shard_map/pallas_call | solution.py:144
  123.4 2.1 %collective-permute-done.14 = f32[136,128]{1,0:T(8,128)S(1)} collective-permute-done((f32[136,128]{1,0:T(8,128)}, f32[136,128]{1,0:T(8,128)S(1)}, u32[]{:S(2)}, u32[]{:S(2)}) %collective-permute-start.14) | collective-permute-done | bytes 69664 | tf_op jit(solution)/shard_map/ppermute | solution.py:154
  125.6 1.6 collective-permute-done.15
  128.2 16.6 %all_to_all.16.msg = f32[8,136,128]{2,1,0:T(8,128)} all-to-all(f32[8,136,128]{2,1,0:T(8,128)S(1)} %broadcast_in_dim.450), channel_id=1, replica_groups={{0,1,2,3,4,5,6,7},{8,9,10,11,12,13,14,15},{16,17,18,19,20,21,22,23},{24..., dimensions={0} | all-to-all | bytes 1114112 | tf_op jit(solution)/shard_map/all_to_all | solution.py:167
  144.8 5.4 %shard_map.100 = (f32[72,128]{1,0:T(8,128)}, f32[128,128]{1,0:T(8,128)}, f32[8,128]{1,0:T(8,128)}) custom-call(s32[1,1,64]{2,1,0:T(1,128)} %src_ids.11, s32[1,1,64]{2,1,0:T(1,128)} %tgt_ids.11, s32[1,1]{1,0:T(1,128)S(6)} %copy.22.count, f32[8,136,128]{2,1,0:T(8,128)} %all_to_all.16.msg, s32[128,128]{1,0:T(8,128)} %bitcast.41, ...), custom_call_target="tpu_custom_call" | custom-call | tf_op jit(solution)/shard_map/pallas_call | solution.py:144
  150.2 3.6 %collective-permute-start.17 = (f32[72,128]{1,0:T(8,128)}, f32[72,128]{1,0:T(8,128)S(1)}, u32[]{:S(2)}, u32[]{:S(2)}) collective-permute-start(f32[72,128]{1,0:T(8,128)} %get-tuple-element.23), channel_id=1, source_target_pairs={{0,32},{32,0},{64,96},{96,64},{128,160},{160,128},{192,224},{224,1... | collective-permute-start | bytes 110600 | tf_op jit(solution)/shard_map/ppermute | solution.py:171
  157.1 1.3 collective-permute-start.19
  160.1 1.5 collective-permute-done.19
  (145 shorter events, 33.3 us)
Async XLA Ops:
  0.7 4.1 %copy-start.10 = (pred[16]{0:T(512)(128)(4,1)}, pred[16]{0:T(512)(128)(4,1)S(1)}, u32[]{:S(2)}) copy-start(pred[16]{0:T(512)(128)(4,1)S(1)} %get-tuple-element.44) | copy-start | bytes 52
  0.7 4.2 %copy-start.13 = (pred[16]{0:T(512)(128)(4,1)}, pred[16]{0:T(512)(128)(4,1)S(1)}, u32[]{:S(2)}) copy-start(pred[16]{0:T(512)(128)(4,1)S(1)} %get-tuple-element.45) | copy-start | bytes 52
  0.7 4.3 %copy-start.16 = (pred[16]{0:T(512)(128)(4,1)}, pred[16]{0:T(512)(128)(4,1)S(1)}, u32[]{:S(2)}) copy-start(pred[16]{0:T(512)(128)(4,1)S(1)} %iota_compare_fusion.6) | copy-start | bytes 52
  4.5 4.0 %copy-start.19 = (pred[128]{0:T(512)(128)(4,1)}, pred[128]{0:T(512)(128)(4,1)S(1)}, u32[]{:S(2)}) copy-start(pred[128]{0:T(512)(128)(4,1)S(1)} %broadcast_in_dim.403) | copy-start | bytes 388
  4.6 3.9 %copy-start.21 = (pred[128]{0:T(512)(128)(4,1)}, pred[128]{0:T(512)(128)(4,1)S(1)}, u32[]{:S(2)}) copy-start(pred[128]{0:T(512)(128)(4,1)S(1)} %broadcast_in_dim.398) | copy-start | bytes 388
  4.7 3.8 %copy-start.23 = (pred[128]{0:T(512)(128)(4,1)}, pred[128]{0:T(512)(128)(4,1)S(1)}, u32[]{:S(2)}) copy-start(pred[128]{0:T(512)(128)(4,1)S(1)} %broadcast_in_dim.393) | copy-start | bytes 388
  4.8 3.7 %copy-start.25 = (pred[128]{0:T(512)(128)(4,1)}, pred[128]{0:T(512)(128)(4,1)S(1)}, u32[]{:S(2)}) copy-start(pred[128]{0:T(512)(128)(4,1)S(1)} %broadcast_in_dim.388) | copy-start | bytes 388
  4.9 3.6 %copy-start.27 = (pred[128]{0:T(512)(128)(4,1)}, pred[128]{0:T(512)(128)(4,1)S(1)}, u32[]{:S(2)}) copy-start(pred[128]{0:T(512)(128)(4,1)S(1)} %broadcast_in_dim.383) | copy-start | bytes 388
  14.5 5.3 %collective-permute-start.2 = (f32[136,128]{1,0:T(8,128)}, f32[136,128]{1,0:T(8,128)S(1)}, u32[]{:S(2)}, u32[]{:S(2)}) collective-permute-start(f32[136,128]{1,0:T(8,128)} %shard_map.95), channel_id=1, source_target_pairs={{0,24},{1,25},{2,26},{3,27},{4,28},{5,29},{6,30},{7,31},{8,0},{9,1... | collective-permute-start | bytes 208904 | tf_op jit(solution)/shard_map/ppermute | solution.py:154
  17.7 7.1 %collective-permute-start = (f32[136,128]{1,0:T(8,128)}, f32[136,128]{1,0:T(8,128)S(1)}, u32[]{:S(2)}, u32[]{:S(2)}) collective-permute-start(f32[136,128]{1,0:T(8,128)} %shard_map.95), channel_id=1, source_target_pairs={{0,8},{1,9},{2,10},{3,11},{4,12},{5,13},{6,14},{7,15},{8,16},{9,17... | collective-permute-start | bytes 208904 | tf_op jit(solution)/shard_map/ppermute | solution.py:154
  17.7 7.1 %collective-permute-start.1 = (f32[136,128]{1,0:T(8,128)}, f32[136,128]{1,0:T(8,128)S(1)}, u32[]{:S(2)}, u32[]{:S(2)}) collective-permute-start(f32[136,128]{1,0:T(8,128)} %shard_map.95), channel_id=1, source_target_pairs={{0,16},{1,17},{2,18},{3,19},{4,20},{5,21},{6,22},{7,23},{8,24},{9,... | collective-permute-start | bytes 208904 | tf_op jit(solution)/shard_map/ppermute | solution.py:154
  26.6 26.4 %all-to-all-start = ((f32[8,136,128]{2,1,0:T(8,128)}), f32[8,136,128]{2,1,0:T(8,128)}, u32[]{:S(2)}, u32[]{:S(2)}) async-start(f32[8,136,128]{2,1,0:T(8,128)} %broadcast_in_dim.420), calls=%async_computation | async-start | bytes 1114112 | tf_op jit(solution)/shard_map/all_to_all | solution.py:167
  58.9 1.4 collective-permute-start.3
  61.2 5.4 %copy-start.2 = (f32[72,128]{1,0:T(8,128)}, f32[72,128]{1,0:T(8,128)S(1)}, u32[]{:S(2)}) copy-start(f32[72,128]{1,0:T(8,128)S(1)} %log_add_fusion.5.m0) | copy-start | bytes 110596
  61.2 4.1 %collective-permute-start.4 = (f32[72,128]{1,0:T(8,128)S(1)}, f32[72,128]{1,0:T(8,128)S(1)}, u32[]{:S(2)}, u32[]{:S(2)}) collective-permute-start(f32[72,128]{1,0:T(8,128)S(1)} %log_add_fusion.5.m0), channel_id=1, source_target_pairs={{0,64},{32,96},{64,128},{96,160},{128,192},{160,224},{192,0},{224,... | collective-permute-start | bytes 110600 | tf_op jit(solution)/shard_map/ppermute | solution.py:158
  61.3 4.4 %collective-permute-start.5 = (f32[72,128]{1,0:T(8,128)S(1)}, f32[72,128]{1,0:T(8,128)S(1)}, u32[]{:S(2)}, u32[]{:S(2)}) collective-permute-start(f32[72,128]{1,0:T(8,128)S(1)} %log_add_fusion.5.m0), channel_id=1, source_target_pairs={{0,128},{32,160},{64,192},{96,224},{128,0},{160,32},{192,64},{224,... | collective-permute-start | bytes 110600 | tf_op jit(solution)/shard_map/ppermute | solution.py:158
  62.3 4.2 %collective-permute-start.6 = (f32[72,128]{1,0:T(8,128)S(1)}, f32[72,128]{1,0:T(8,128)S(1)}, u32[]{:S(2)}, u32[]{:S(2)}) collective-permute-start(f32[72,128]{1,0:T(8,128)S(1)} %log_add_fusion.5.m0), channel_id=1, source_target_pairs={{0,192},{32,224},{64,0},{96,32},{128,64},{160,96},{192,128},{224,1... | collective-permute-start | bytes 110600 | tf_op jit(solution)/shard_map/ppermute | solution.py:158
  72.6 4.1 %collective-permute-start.9 = (f32[136,128]{1,0:T(8,128)}, f32[136,128]{1,0:T(8,128)S(1)}, u32[]{:S(2)}, u32[]{:S(2)}) collective-permute-start(f32[136,128]{1,0:T(8,128)} %get-tuple-element.15), channel_id=1, source_target_pairs={{0,24},{1,25},{2,26},{3,27},{4,28},{5,29},{6,30},{7,31},{8,0},{9,1... | collective-permute-start | bytes 208904 | tf_op jit(solution)/shard_map/ppermute | solution.py:154
  73.3 4.6 %collective-permute-start.7 = (f32[136,128]{1,0:T(8,128)}, f32[136,128]{1,0:T(8,128)S(1)}, u32[]{:S(2)}, u32[]{:S(2)}) collective-permute-start(f32[136,128]{1,0:T(8,128)} %get-tuple-element.15), channel_id=1, source_target_pairs={{0,8},{1,9},{2,10},{3,11},{4,12},{5,13},{6,14},{7,15},{8,16},{9,17... | collective-permute-start | bytes 208904 | tf_op jit(solution)/shard_map/ppermute | solution.py:154
  74.0 5.1 %collective-permute-start.8 = (f32[136,128]{1,0:T(8,128)}, f32[136,128]{1,0:T(8,128)S(1)}, u32[]{:S(2)}, u32[]{:S(2)}) collective-permute-start(f32[136,128]{1,0:T(8,128)} %get-tuple-element.15), channel_id=1, source_target_pairs={{0,16},{1,17},{2,18},{3,19},{4,20},{5,21},{6,22},{7,23},{8,24},{9,... | collective-permute-start | bytes 208904 | tf_op jit(solution)/shard_map/ppermute | solution.py:154
  102.6 4.2 %collective-permute-start.10 = (f32[72,128]{1,0:T(8,128)}, f32[72,128]{1,0:T(8,128)S(1)}, u32[]{:S(2)}, u32[]{:S(2)}) collective-permute-start(f32[72,128]{1,0:T(8,128)} %get-tuple-element.17), channel_id=1, source_target_pairs={{0,32},{32,0},{64,96},{96,64},{128,160},{160,128},{192,224},{224,1... | collective-permute-start | bytes 110600 | tf_op jit(solution)/shard_map/ppermute | solution.py:171
  107.6 6.6 %copy-start.1 = (f32[72,128]{1,0:T(8,128)}, f32[72,128]{1,0:T(8,128)S(1)}, u32[]{:S(2)}) copy-start(f32[72,128]{1,0:T(8,128)S(1)} %log_add_fusion.4.m0) | copy-start | bytes 110596
  107.6 4.1 %collective-permute-start.11 = (f32[72,128]{1,0:T(8,128)S(1)}, f32[72,128]{1,0:T(8,128)S(1)}, u32[]{:S(2)}, u32[]{:S(2)}) collective-permute-start(f32[72,128]{1,0:T(8,128)S(1)} %log_add_fusion.4.m0), channel_id=1, source_target_pairs={{0,64},{32,96},{64,128},{96,160},{128,192},{160,224},{192,0},{224,... | collective-permute-start | bytes 110600 | tf_op jit(solution)/shard_map/ppermute | solution.py:158
  107.7 5.4 %collective-permute-start.12 = (f32[72,128]{1,0:T(8,128)S(1)}, f32[72,128]{1,0:T(8,128)S(1)}, u32[]{:S(2)}, u32[]{:S(2)}) collective-permute-start(f32[72,128]{1,0:T(8,128)S(1)} %log_add_fusion.4.m0), channel_id=1, source_target_pairs={{0,128},{32,160},{64,192},{96,224},{128,0},{160,32},{192,64},{224,... | collective-permute-start | bytes 110600 | tf_op jit(solution)/shard_map/ppermute | solution.py:158
  111.4 2.8 %collective-permute-start.13 = (f32[72,128]{1,0:T(8,128)S(1)}, f32[72,128]{1,0:T(8,128)S(1)}, u32[]{:S(2)}, u32[]{:S(2)}) collective-permute-start(f32[72,128]{1,0:T(8,128)S(1)} %log_add_fusion.4.m0), channel_id=1, source_target_pairs={{0,192},{32,224},{64,0},{96,32},{128,64},{160,96},{192,128},{224,1... | collective-permute-start | bytes 110600 | tf_op jit(solution)/shard_map/ppermute | solution.py:158
  120.1 3.4 %collective-permute-start.16 = (f32[136,128]{1,0:T(8,128)}, f32[136,128]{1,0:T(8,128)S(1)}, u32[]{:S(2)}, u32[]{:S(2)}) collective-permute-start(f32[136,128]{1,0:T(8,128)} %get-tuple-element.19), channel_id=1, source_target_pairs={{0,24},{1,25},{2,26},{3,27},{4,28},{5,29},{6,30},{7,31},{8,0},{9,1... | collective-permute-start | bytes 208904 | tf_op jit(solution)/shard_map/ppermute | solution.py:154
  121.0 4.6 %collective-permute-start.14 = (f32[136,128]{1,0:T(8,128)}, f32[136,128]{1,0:T(8,128)S(1)}, u32[]{:S(2)}, u32[]{:S(2)}) collective-permute-start(f32[136,128]{1,0:T(8,128)} %get-tuple-element.19), channel_id=1, source_target_pairs={{0,8},{1,9},{2,10},{3,11},{4,12},{5,13},{6,14},{7,15},{8,16},{9,17... | collective-permute-start | bytes 208904 | tf_op jit(solution)/shard_map/ppermute | solution.py:154
  121.5 5.6 %collective-permute-start.15 = (f32[136,128]{1,0:T(8,128)}, f32[136,128]{1,0:T(8,128)S(1)}, u32[]{:S(2)}, u32[]{:S(2)}) collective-permute-start(f32[136,128]{1,0:T(8,128)} %get-tuple-element.19), channel_id=1, source_target_pairs={{0,16},{1,17},{2,18},{3,19},{4,20},{5,21},{6,22},{7,23},{8,24},{9,... | collective-permute-start | bytes 208904 | tf_op jit(solution)/shard_map/ppermute | solution.py:154
  150.2 4.6 %collective-permute-start.17 = (f32[72,128]{1,0:T(8,128)}, f32[72,128]{1,0:T(8,128)S(1)}, u32[]{:S(2)}, u32[]{:S(2)}) collective-permute-start(f32[72,128]{1,0:T(8,128)} %get-tuple-element.23), channel_id=1, source_target_pairs={{0,32},{32,0},{64,96},{96,64},{128,160},{160,128},{192,224},{224,1... | collective-permute-start | bytes 110600 | tf_op jit(solution)/shard_map/ppermute | solution.py:171
  155.6 3.5 %collective-permute-start.20 = (f32[72,128]{1,0:T(8,128)S(1)}, f32[72,128]{1,0:T(8,128)S(1)}, u32[]{:S(2)}, u32[]{:S(2)}) collective-permute-start(f32[72,128]{1,0:T(8,128)S(1)} %log_add_fusion.3), channel_id=1, source_target_pairs={{0,192},{32,224},{64,0},{96,32},{128,64},{160,96},{192,128},{224,1... | collective-permute-start | bytes 110600 | tf_op jit(solution)/shard_map/ppermute | solution.py:158
  156.1 4.0 %collective-permute-start.18 = (f32[72,128]{1,0:T(8,128)S(1)}, f32[72,128]{1,0:T(8,128)S(1)}, u32[]{:S(2)}, u32[]{:S(2)}) collective-permute-start(f32[72,128]{1,0:T(8,128)S(1)} %log_add_fusion.3), channel_id=1, source_target_pairs={{0,64},{32,96},{64,128},{96,160},{128,192},{160,224},{192,0},{224,... | collective-permute-start | bytes 110600 | tf_op jit(solution)/shard_map/ppermute | solution.py:158
  157.1 4.4 %collective-permute-start.19 = (f32[72,128]{1,0:T(8,128)S(1)}, f32[72,128]{1,0:T(8,128)S(1)}, u32[]{:S(2)}, u32[]{:S(2)}) collective-permute-start(f32[72,128]{1,0:T(8,128)S(1)} %log_add_fusion.3), channel_id=1, source_target_pairs={{0,128},{32,160},{64,192},{96,224},{128,0},{160,32},{192,64},{224,... | collective-permute-start | bytes 110600 | tf_op jit(solution)/shard_map/ppermute | solution.py:158
  (23 other events, 28.6 us)

commit v2 on v1

v2 whole, which is shorter than its diff:
```python
import functools

import jax
import jax.numpy as jnp
from jax import lax
from jax.experimental import pallas as pl
from jax.experimental.pallas import tpu as pltpu
from jax.sharding import PartitionSpec as P

ITERS = 3
NONE = -1.0e30
UNITS = 20.0
STEP = 0.05
BASE2 = STEP * 1.4426950408889634
SLOTS = 64


def lse(parts):
    top = functools.reduce(jnp.maximum, parts)
    terms = [jnp.exp(p - top) for p in parts]
    while len(terms) > 1:
        half = len(terms) // 2
        terms = [terms[k] + terms[k + half] for k in range(half)]
    return top + jnp.log(terms[0])


def features(coords_ref, rows_ref, left_out, right_out, scratch):
    tiles = coords_ref.shape[1] // 128
    for d in range(3):
        for t in range(tiles):
            rows_ref[d, t : t + 1, :] = coords_ref[d : d + 1, t * 128 : (t + 1) * 128]
    scratch[0 : tiles * 16, :] = jnp.zeros((tiles * 16, 128), jnp.float32)
    for at in range(0, tiles, 8):
        x, y, z = (rows_ref[d, at : at + 8, :] for d in range(3))
        norm = x * x + y * y + z * z
        low = norm & 31
        high = norm - low
        one = jnp.ones((8, 128), jnp.float32)
        if left_out is not None:
            values = [x, y, z, high, low, one, one]
        else:
            values = [-2 * x, -2 * y, -2 * z, one, one, high, low]
        for k, value in enumerate(values):
            scratch[pl.ds(at * 16 + k, 8, stride=16), :] = value.astype(jnp.float32)
    if left_out is not None:
        for c in range(tiles // 8):
            left_out[c] = scratch[c * 128 : (c + 1) * 128, :].T.astype(jnp.bfloat16)
    else:
        for t in range(tiles):
            right_out[t] = scratch[t * 16 : (t + 1) * 16, :].astype(jnp.bfloat16)


def half_step(potential, lane_ids_ref, sub_ids_ref, count_ref, left_ref, right_ref, peaks_ref, totals_ref, tops_ref, sums_ref, out_ref):
    sub_tiles = potential.shape[0]
    lane_tiles = tops_ref.shape[0]
    scaled = potential * UNITS
    if sub_tiles < 128:
        scaled = jnp.concatenate([scaled, jnp.zeros((128 - sub_tiles, 128), jnp.float32)], axis=0)
    columns = scaled.T
    count = count_ref[0, 0]
    ids = [lane_ids_ref[0, 0, k] & (lane_tiles - 1) for k in range(SLOTS)]
    peaks, totals = [], []
    for k in range(SLOTS):
        sub = sub_ids_ref[0, 0, k] & (sub_tiles - 1)
        block = right_ref[ids[k]]
        member = sub & 7
        right = jnp.concatenate(
            [jnp.where(member == q, block, jnp.zeros_like(block)) for q in range(8)], axis=0
        )
        square = jnp.dot(left_ref[sub >> 3], right, preferred_element_type=jnp.float32)
        value = jnp.take_along_axis(columns, jnp.full((128, 128), sub, jnp.int32), axis=1)
        score = value - square
        peak = jnp.max(score, axis=0, keepdims=True)
        totals.append(jnp.sum(jnp.exp2((score - peak) * BASE2), axis=0, keepdims=True))
        peaks.append(jnp.where(k < count, peak * STEP, NONE))
        if k % 8 == 7:
            peaks_ref[k - 7 : k + 1, :] = jnp.concatenate(peaks, axis=0) + jnp.log(jnp.concatenate(totals, axis=0))
            peaks, totals = [], []
    tops_ref[...] = jnp.full(tops_ref.shape, NONE, jnp.float32)
    sums_ref[...] = jnp.zeros(sums_ref.shape, jnp.float32)
    for k in range(SLOTS):
        at = pl.ds(ids[k], 1)
        tops_ref[at, :] = jnp.maximum(tops_ref[at, :], peaks_ref[k : k + 1, :])
    for k in range(SLOTS):
        totals_ref[k : k + 1, :] = jnp.exp(peaks_ref[k : k + 1, :] - tops_ref[pl.ds(ids[k], 1), :])
    for k in range(SLOTS):
        at = pl.ds(ids[k], 1)
        sums_ref[at, :] = sums_ref[at, :] + totals_ref[k : k + 1, :]
    tops = tops_ref[...]
    out_ref[0:lane_tiles, :] = jnp.where(tops > 0.5 * NONE, tops + jnp.log(sums_ref[...]), NONE)


def put_total(out_ref, mass):
    rows = out_ref.shape[0]
    total = jnp.sum(jnp.sum(mass.astype(jnp.float32), axis=0, keepdims=True), axis=1, keepdims=True)
    out_ref[rows - 8 : rows, :] = jnp.broadcast_to(jnp.log(total), (8, 128))


def first_kernel(src_ids, tgt_ids, count, start, tgt_mass, src_coords, tgt_coords, out, left, right, peaks, totals, tops, sums, rows, scratch):
    features(tgt_coords, rows, left, None, scratch)
    features(src_coords, rows, None, right, scratch)
    half_step(start[...], src_ids, tgt_ids, count, left, right, peaks, totals, tops, sums, out)
    put_total(out, tgt_mass[...])


def other_kernel(src_coords, tgt_coords, left, right, rows, scratch):
    features(src_coords, rows, left, None, scratch)
    features(tgt_coords, rows, None, right, scratch)


def src_kernel(is_first, src_ids, tgt_ids, count, msg, src_mass, src_const, left, right, out, pot_ref, const_ref, peaks, totals, tops, sums):
    merged = lse([msg[k] for k in range(msg.shape[0])])
    const_ref[...] = merged[128:136]
    potential = jnp.log(src_mass[...].astype(jnp.float32)) - merged[0:128]
    if not is_first:
        potential = potential - src_const[0:1]
    pot_ref[...] = potential
    half_step(potential, tgt_ids, src_ids, count, left, right, peaks, totals, tops, sums, out)
    put_total(out, src_mass[...])


def tgt_value(is_first, parts, tgt_mass, tgt_const):
    merged = lse(parts)
    const = merged[64:72]
    potential = jnp.log(tgt_mass.astype(jnp.float32)) - tgt_const[0:1] - merged[0:64]
    if is_first:
        potential = potential + const[0:1]
    return potential, const


def tgt_kernel(is_first, src_ids, tgt_ids, count, m0, m1, m2, m3, tgt_mass, tgt_const, left, right, out, const_ref, peaks, totals, tops, sums):
    potential, const = tgt_value(is_first, [m0[...], m1[...], m2[...], m3[...]], tgt_mass[...], tgt_const[...])
    const_ref[...] = const
    half_step(potential, src_ids, tgt_ids, count, left, right, peaks, totals, tops, sums, out)
    put_total(out, tgt_mass[...])


SMEM = pl.BlockSpec(memory_space=pltpu.SMEM)
VMEM = pl.BlockSpec(memory_space=pltpu.VMEM)


F32 = jnp.float32
FEATURE_SCRATCH = [pltpu.VMEM((3, 128, 128), jnp.int32), pltpu.VMEM((2048, 128), F32)]
PARAMS = pltpu.CompilerParams(vmem_limit_bytes=8 << 20)


def call(body, lane_tiles, extra_outs, *args, scratch=()):
    shapes = [jax.ShapeDtypeStruct((lane_tiles + 8, 128), F32)] + [jax.ShapeDtypeStruct(*s) for s in extra_outs]
    return pl.pallas_call(
        body,
        out_shape=shapes,
        in_specs=[SMEM] * 3 + [VMEM] * (len(args) - 3),
        out_specs=[VMEM] * len(shapes),
        scratch_shapes=[pltpu.VMEM((SLOTS, 128), F32)] * 2 + [pltpu.VMEM((lane_tiles, 128), F32)] * 2 + list(scratch),
        compiler_params=PARAMS,
    )(*args)


def feature_shapes(left_tiles, right_tiles):
    return [((left_tiles // 8, 128, 128), jnp.bfloat16), ((right_tiles, 16, 128), jnp.bfloat16)]


def other_features(src_coords, tgt_coords):
    shapes = [jax.ShapeDtypeStruct(*s) for s in feature_shapes(128, 64)]
    return pl.pallas_call(
        other_kernel, out_shape=shapes, in_specs=[VMEM] * 2, out_specs=[VMEM] * 2,
        scratch_shapes=FEATURE_SCRATCH, compiler_params=PARAMS,
    )(src_coords, tgt_coords)


def col_permute(value, shift):
    return lax.ppermute(value, "col", [(i, (i // 8 + shift) % 4 * 8 + i % 8) for i in range(32)])


def row_permute(value, shift):
    return lax.ppermute(value, "row", [(i, (i + 2 * shift) % 8) for i in range(8)])


Z_GROUPS = [[y * 8 + z for z in range(8)] for y in range(4)]


def over_col(message):
    merged = lse([message] + [col_permute(message, k) for k in (1, 2, 3)])
    copies = jnp.broadcast_to(merged[None], (8,) + merged.shape)
    return lax.all_to_all(copies, "col", 0, 0, tiled=True, axis_index_groups=Z_GROUPS)


def over_row(message):
    other = lax.ppermute(message, "row", [(i, i ^ 1) for i in range(8)])
    merged = lse([message, other])
    return [merged] + [row_permute(merged, k) for k in (1, 2, 3)]


def on_device(src_coords, tgt_coords, src_mass, tgt_mass, tgt_start, kept_src, kept_tgt, kept_count):
    src_mass = src_mass.reshape(128, 128)
    tgt_mass = tgt_mass.reshape(64, 128)
    lists = (kept_src, kept_tgt, kept_count)
    message, tgt_left, src_right = call(
        first_kernel, 128, feature_shapes(64, 128),
        *lists, tgt_start.reshape(64, 128), tgt_mass, src_coords, tgt_coords, scratch=FEATURE_SCRATCH,
    )
    src_left, tgt_right = other_features(src_coords, tgt_coords)
    src_const = jnp.zeros((8, 128), F32)
    src_potential = None
    for iteration in range(ITERS):
        first = iteration == 0
        messages = over_col(message)
        message, src_potential, tgt_const = call(
            functools.partial(src_kernel, first), 64, [((128, 128), F32), ((8, 128), F32)],
            *lists, messages, src_mass, src_const, src_left, tgt_right,
        )
        parts = over_row(message)
        if iteration + 1 < ITERS:
            message, src_const = call(
                functools.partial(tgt_kernel, first), 128, [((8, 128), F32)],
                *lists, *parts, tgt_mass, tgt_const, tgt_left, src_right,
            )
    tgt_potential, _ = tgt_value(False, parts, tgt_mass, tgt_const)
    return src_potential.reshape(-1), tgt_potential.reshape(-1)


def solution(mesh):
    placed = (
        P(None, "row"),
        P(None, "col"),
        P("row"),
        P("col"),
        P("col"),
        P("row", "col", None),
        P("row", "col", None),
        P("row", "col"),
    )
    return jax.shard_map(
        on_device, mesh=mesh, in_specs=placed, out_specs=(P("row"), P("col")), check_vma=False
    )
```

time: 164 us -> 142 us (0.87)
  Pallas kernels: 32 us -> 20 us
  other arithmetic: 12.9 us -> 0.97 us
  local copies, waits for them, and re-layouts: 14.1 us -> 4.96 us
  starting transfers between devices: 32.2 us -> 39 us
  waiting for transfers between devices: 35.6 us -> 42.2 us
    pallas_call x6 -> x7, Pallas kernels: 32 us -> 20 us  [the longest x6 19.4 us: call(): pl.pallas_call(body, out_shape=shapes, in_specs=[SMEM] * 3 + [VMEM] * (le...]
    broadcast_in_dim x35 -> x1, local copies, waits for them, and re-layouts: 7.42 us -> 0.01 us  [on_device(): src_const = jnp.zeros((8, 128), F32)]
    all_to_all x1, waiting for transfers between devices: 8.77 us -> 15.8 us  [over_col(): lax.all_to_all(copies, 'col', 0, 0, tiled=True, axis_index_groups=Z_GROUPS)]
    ppermute x3, starting transfers between devices: 6.72 us -> 12.7 us  [over_row(): other = lax.ppermute(message, 'row', [(i, i ^ 1) for i in range(8)])]
    add x6, other arithmetic: 5.26 us -> 0.3 us  [lse(): return top + jnp.log(terms[0])]
    transpose x2 -> x0, other arithmetic: 4.07 us -> none  [features(): left = left.reshape(-1, 128, 128).transpose(0, 2, 1)]
    ppermute x9, waiting for transfers between devices: 7.9 us -> 11.2 us  [row_permute(): lax.ppermute(value, 'row', [(i, (i + 2 * shift) % 8) for i in range(8)])]
    ppermute x9, waiting for transfers between devices: 15.3 us -> 12.7 us  [col_permute(): lax.ppermute(value, 'col', [(i, (i // 8 + shift) % 4 * 8 + i % 8) for i i...]
  transfers between devices with their start and end apart: 22 -> 22, of which waited for: 20 -> 21; matrix products, arithmetic and copies ran while one was open for 6% -> 0% of each run, Pallas kernels for 0% -> 0%
where the time goes in v2:
time: 142 us
  waiting for transfers between devices  42.2 us (30%)
  starting transfers between devices  39 us (27%)
  blocking collectives  33.1 us (23%)
  Pallas kernels  20 us (14%)
  local copies, waits for them, and re-layouts  4.96 us (3%)
    all_to_all x2, blocking collectives, over_col(): lax.all_to_all(copies, 'col', 0, 0, tiled=True, axis_index_groups=Z_GROUPS)  33.1 us
    pallas_call x6, Pallas kernels, call(): pl.pallas_call(body, out_shape=shapes, in_specs=[SMEM] * 3 + [VMEM] * (le...  19.4 us
    all_to_all x1, waiting for transfers between devices, over_col(): lax.all_to_all(copies, 'col', 0, 0, tiled=True, axis_index_groups=Z_GROUPS)  15.8 us
    ppermute x9, waiting for transfers between devices, col_permute(): lax.ppermute(value, 'col', [(i, (i // 8 + shift) % 4 * 8 + i % 8) for i i...  12.7 us
    ppermute x3, starting transfers between devices, over_row(): other = lax.ppermute(message, 'row', [(i, i ^ 1) for i in range(8)])  12.7 us
    ppermute x9, waiting for transfers between devices, row_permute(): lax.ppermute(value, 'row', [(i, (i + 2 * shift) % 8) for i in range(8)])  11.2 us
    ppermute x9, starting transfers between devices, col_permute(): lax.ppermute(value, 'col', [(i, (i // 8 + shift) % 4 * 8 + i % 8) for i i...  9.85 us
    all_to_all x1, starting transfers between devices, over_col(): lax.all_to_all(copies, 'col', 0, 0, tiled=True, axis_index_groups=Z_GROUPS)  8.33 us
  transfers between devices with their start and end apart: 22, of which 21 were waited for; matrix products, arithmetic and copies ran while one was open for 0% of the time, Pallas kernels for 0%

profile of v2, /device:TPU:1, one launch (start us, length us, event | category | flops | bytes accessed | tf_op | source)
XLA Modules:
  0.0 141.7 jit_solution(7586595881388058890)
XLA Ops:
  2.0 0.9 copy-done
  3.7 0.9 copy-done.5
  5.3 3.4 %shard_map.95 = (f32[136,128]{1,0:T(8,128)S(1)}, bf16[8,128,128]{2,1,0:T(8,128)(2,1)S(1)}, bf16[128,16,128]{2,1,0:T(8,128)(2,1)S(1)}) custom-call(s32[1,1,64]{2,1,0:T(1,128)S(1)} %copy-done.8, s32[1,1,64]{2,1,0:T(1,128)S(1)} %copy-done.9, s32[1,1]{1,0:T(1,128)S(6)} %copy.10.count, f32[64,128]{1,0:T(8,128)S(1)} %bitcast.15, s32[64,128]{1,0:T(8,128)S(1)} %bitcast.12, ...), custom_call_target="tpu_custom_call" | custom-call | tf_op jit(solution)/shard_map/pallas_call | solution.py:149
  8.7 3.6 %collective-permute-start.2 = (f32[136,128]{1,0:T(8,128)S(1)}, f32[136,128]{1,0:T(8,128)S(1)}, u32[]{:S(2)}, u32[]{:S(2)}) collective-permute-start(f32[136,128]{1,0:T(8,128)S(1)} %get-tuple-element.18), channel_id=1, source_target_pairs={{0,24},{1,25},{2,26},{3,27},{4,28},{5,29},{6,30},{7,31},{8,0},{9,1... | collective-permute-start | bytes 208904 | tf_op jit(solution)/shard_map/ppermute | solution.py:172
  13.7 3.4 %collective-permute-done.1 = f32[136,128]{1,0:T(8,128)S(1)} collective-permute-done((f32[136,128]{1,0:T(8,128)S(1)}, f32[136,128]{1,0:T(8,128)S(1)}, u32[]{:S(2)}, u32[]{:S(2)}) %collective-permute-start.1) | collective-permute-done | bytes 69664 | tf_op jit(solution)/shard_map/ppermute | solution.py:172
  17.1 1.0 collective-permute-done
  19.0 8.3 %all-to-all-start = ((f32[8,136,128]{2,1,0:T(8,128)}), f32[8,136,128]{2,1,0:T(8,128)S(1)}, u32[]{:S(2)}, u32[]{:S(2)}) async-start(f32[8,136,128]{2,1,0:T(8,128)} %broadcast_in_dim.8), calls=%async_computation | async-start | bytes 1114112 | tf_op jit(solution)/shard_map/all_to_all | solution.py:185
  27.9 15.8 %all-to-all-done.msg = f32[8,136,128]{2,1,0:T(8,128)S(1)} async-done(((f32[8,136,128]{2,1,0:T(8,128)}), f32[8,136,128]{2,1,0:T(8,128)S(1)}, u32[]{:S(2)}, u32[]{:S(2)}) %all-to-all-start) | async-done | bytes 557088 | tf_op jit(solution)/shard_map/all_to_all | solution.py:185
  43.7 3.5 %shard_map.97 = (f32[72,128]{1,0:T(8,128)S(1)}, f32[128,128]{1,0:T(8,128)}, f32[8,128]{1,0:T(8,128)S(1)}) custom-call(s32[1,1,64]{2,1,0:T(1,128)S(1)} %copy-done.8, s32[1,1,64]{2,1,0:T(1,128)S(1)} %copy-done.9, s32[1,1]{1,0:T(1,128)S(6)} %copy.10.count, f32[8,136,128]{2,1,0:T(8,128)S(1)} %all-to-all-done.msg, s32[128,128]{1,0:T(8,128)S(1)} %bitcast.9, ...), custom_call_target="tpu_custom_call" | custom-call | tf_op jit(solution)/shard_map/pallas_call | solution.py:149
  47.2 2.8 %collective-permute-start.3 = (f32[72,128]{1,0:T(8,128)S(1)}, f32[72,128]{1,0:T(8,128)S(1)}, u32[]{:S(2)}, u32[]{:S(2)}) collective-permute-start(f32[72,128]{1,0:T(8,128)S(1)} %get-tuple-element.21), channel_id=1, source_target_pairs={{0,32},{32,0},{64,96},{96,64},{128,160},{160,128},{192,224},{224,1... | collective-permute-start | bytes 110600 | tf_op jit(solution)/shard_map/ppermute | solution.py:189
  50.8 2.5 %collective-permute-start.6 = (f32[72,128]{1,0:T(8,128)S(1)}, f32[72,128]{1,0:T(8,128)S(1)}, u32[]{:S(2)}, u32[]{:S(2)}) collective-permute-start(f32[72,128]{1,0:T(8,128)S(1)} %log_add_fusion.5.m0), channel_id=1, source_target_pairs={{0,192},{32,224},{64,0},{96,32},{128,64},{160,96},{192,128},{224,1... | collective-permute-start | bytes 110600 | tf_op jit(solution)/shard_map/ppermute | solution.py:176
  54.5 3.2 %collective-permute-done.5.m2 = f32[72,128]{1,0:T(8,128)S(1)} collective-permute-done((f32[72,128]{1,0:T(8,128)S(1)}, f32[72,128]{1,0:T(8,128)S(1)}, u32[]{:S(2)}, u32[]{:S(2)}) %collective-permute-start.5) | collective-permute-done | bytes 36896 | tf_op jit(solution)/shard_map/ppermute | solution.py:176
  58.1 2.8 %shard_map.98 = (f32[136,128]{1,0:T(8,128)S(1)}, f32[8,128]{1,0:T(8,128)S(1)}) custom-call(s32[1,1,64]{2,1,0:T(1,128)S(1)} %copy-done.8, s32[1,1,64]{2,1,0:T(1,128)S(1)} %copy-done.9, s32[1,1]{1,0:T(1,128)S(6)} %copy.10.count, f32[72,128]{1,0:T(8,128)S(1)} %log_add_fusion.5.m0, f32[72,128]{1,0:T(8,128)S(1)} %collective-permute-done.4.m1, ...), custom_call_target="tpu_custom_call" | custom-call | tf_op jit(solution)/shard_map/pallas_call | solution.py:149
  61.3 1.0 collective-permute-start.8
  63.0 1.2 collective-permute-done.9
  64.2 1.8 %collective-permute-done.8 = f32[136,128]{1,0:T(8,128)S(1)} collective-permute-done((f32[136,128]{1,0:T(8,128)S(1)}, f32[136,128]{1,0:T(8,128)S(1)}, u32[]{:S(2)}, u32[]{:S(2)}) %collective-permute-start.8) | collective-permute-done | bytes 69664 | tf_op jit(solution)/shard_map/ppermute | solution.py:172
  66.8 16.2 %all_to_all.15.msg = f32[8,136,128]{2,1,0:T(8,128)S(1)} all-to-all(f32[8,136,128]{2,1,0:T(8,128)S(1)} %broadcast_in_dim.10), channel_id=1, replica_groups={{0,1,2,3,4,5,6,7},{8,9,10,11,12,13,14,15},{16,17,18,19,20,21,22,23},{24..., dimensions={0} | all-to-all | bytes 1114112 | tf_op jit(solution)/shard_map/all_to_all | solution.py:185
  83.0 3.5 %shard_map.99 = (f32[72,128]{1,0:T(8,128)S(1)}, f32[128,128]{1,0:T(8,128)}, f32[8,128]{1,0:T(8,128)S(1)}) custom-call(s32[1,1,64]{2,1,0:T(1,128)S(1)} %copy-done.8, s32[1,1,64]{2,1,0:T(1,128)S(1)} %copy-done.9, s32[1,1]{1,0:T(1,128)S(6)} %copy.10.count, f32[8,136,128]{2,1,0:T(8,128)S(1)} %all_to_all.15.msg, s32[128,128]{1,0:T(8,128)S(1)} %bitcast.10, ...), custom_call_target="tpu_custom_call" | custom-call | tf_op jit(solution)/shard_map/pallas_call | solution.py:149
  86.5 5.3 %collective-permute-start.10 = (f32[72,128]{1,0:T(8,128)S(1)}, f32[72,128]{1,0:T(8,128)S(1)}, u32[]{:S(2)}, u32[]{:S(2)}) collective-permute-start(f32[72,128]{1,0:T(8,128)S(1)} %get-tuple-element.27), channel_id=1, source_target_pairs={{0,32},{32,0},{64,96},{96,64},{128,160},{160,128},{192,224},{224,1... | collective-permute-start | bytes 110600 | tf_op jit(solution)/shard_map/ppermute | solution.py:189
  93.3 1.0 collective-permute-start.12
  95.6 2.1 %collective-permute-done.12.m2 = f32[72,128]{1,0:T(8,128)S(1)} collective-permute-done((f32[72,128]{1,0:T(8,128)S(1)}, f32[72,128]{1,0:T(8,128)S(1)}, u32[]{:S(2)}, u32[]{:S(2)}) %collective-permute-start.12) | collective-permute-done | bytes 36896 | tf_op jit(solution)/shard_map/ppermute | solution.py:176
  97.6 1.0 collective-permute-done.11.m1
  98.7 2.8 %shard_map.100 = (f32[136,128]{1,0:T(8,128)S(1)}, f32[8,128]{1,0:T(8,128)S(1)}) custom-call(s32[1,1,64]{2,1,0:T(1,128)S(1)} %copy-done.8, s32[1,1,64]{2,1,0:T(1,128)S(1)} %copy-done.9, s32[1,1]{1,0:T(1,128)S(6)} %copy.10.count, f32[72,128]{1,0:T(8,128)S(1)} %log_add_fusion.4.m0, f32[72,128]{1,0:T(8,128)S(1)} %collective-permute-done.11.m1, ...), custom_call_target="tpu_custom_call" | custom-call | tf_op jit(solution)/shard_map/pallas_call | solution.py:149
  101.5 1.7 %collective-permute-start.16 = (f32[136,128]{1,0:T(8,128)S(1)}, f32[136,128]{1,0:T(8,128)S(1)}, u32[]{:S(2)}, u32[]{:S(2)}) collective-permute-start(f32[136,128]{1,0:T(8,128)S(1)} %get-tuple-element.29), channel_id=1, source_target_pairs={{0,24},{1,25},{2,26},{3,27},{4,28},{5,29},{6,30},{7,31},{8,0},{9,1... | collective-permute-start | bytes 208904 | tf_op jit(solution)/shard_map/ppermute | solution.py:172
  103.2 1.5 %collective-permute-start.15 = (f32[136,128]{1,0:T(8,128)S(1)}, f32[136,128]{1,0:T(8,128)S(1)}, u32[]{:S(2)}, u32[]{:S(2)}) collective-permute-start(f32[136,128]{1,0:T(8,128)S(1)} %get-tuple-element.29), channel_id=1, source_target_pairs={{0,16},{1,17},{2,18},{3,19},{4,20},{5,21},{6,22},{7,23},{8,24},{9,... | collective-permute-start | bytes 208904 | tf_op jit(solution)/shard_map/ppermute | solution.py:172
  104.9 2.9 %collective-permute-done.15 = f32[136,128]{1,0:T(8,128)S(1)} collective-permute-done((f32[136,128]{1,0:T(8,128)S(1)}, f32[136,128]{1,0:T(8,128)S(1)}, u32[]{:S(2)}, u32[]{:S(2)}) %collective-permute-start.15) | collective-permute-done | bytes 69664 | tf_op jit(solution)/shard_map/ppermute | solution.py:172
  107.8 1.2 collective-permute-done.14
  109.1 16.9 %all_to_all.16.msg = f32[8,136,128]{2,1,0:T(8,128)S(1)} all-to-all(f32[8,136,128]{2,1,0:T(8,128)S(1)} %broadcast_in_dim.11), channel_id=1, replica_groups={{0,1,2,3,4,5,6,7},{8,9,10,11,12,13,14,15},{16,17,18,19,20,21,22,23},{24..., dimensions={0} | all-to-all | bytes 1114112 | tf_op jit(solution)/shard_map/all_to_all | solution.py:185
  126.0 3.5 %shard_map.101 = (f32[72,128]{1,0:T(8,128)S(1)}, f32[128,128]{1,0:T(8,128)}, f32[8,128]{1,0:T(8,128)S(1)}) custom-call(s32[1,1,64]{2,1,0:T(1,128)S(1)} %copy-done.8, s32[1,1,64]{2,1,0:T(1,128)S(1)} %copy-done.9, s32[1,1]{1,0:T(1,128)S(6)} %copy.10.count, f32[8,136,128]{2,1,0:T(8,128)S(1)} %all_to_all.16.msg, s32[128,128]{1,0:T(8,128)S(1)} %bitcast.11, ...), custom_call_target="tpu_custom_call" | custom-call | tf_op jit(solution)/shard_map/pallas_call | solution.py:149
  129.5 4.6 %collective-permute-start.17 = (f32[72,128]{1,0:T(8,128)S(1)}, f32[72,128]{1,0:T(8,128)S(1)}, u32[]{:S(2)}, u32[]{:S(2)}) collective-permute-start(f32[72,128]{1,0:T(8,128)S(1)} %get-tuple-element.33), channel_id=1, source_target_pairs={{0,32},{32,0},{64,96},{96,64},{128,160},{160,128},{192,224},{224,1... | collective-permute-start | bytes 110600 | tf_op jit(solution)/shard_map/ppermute | solution.py:189
  135.0 1.3 collective-permute-start.20
  137.9 2.8 %collective-permute-done.19 = f32[72,128]{1,0:T(8,128)S(1)} collective-permute-done((f32[72,128]{1,0:T(8,128)S(1)}, f32[72,128]{1,0:T(8,128)S(1)}, u32[]{:S(2)}, u32[]{:S(2)}) %collective-permute-start.19) | collective-permute-done | bytes 36896 | tf_op jit(solution)/shard_map/ppermute | solution.py:176
  (54 shorter events, 16.1 us)
Async XLA Ops:
  1.3 0.7 copy-start.8
  1.3 0.7 copy-start.9
  1.9 0.9 copy-start
  2.9 0.8 copy-start.3
  3.7 0.9 copy-start.5
  4.6 0.8 copy-start.7
  8.7 5.0 %collective-permute-start.2 = (f32[136,128]{1,0:T(8,128)S(1)}, f32[136,128]{1,0:T(8,128)S(1)}, u32[]{:S(2)}, u32[]{:S(2)}) collective-permute-start(f32[136,128]{1,0:T(8,128)S(1)} %get-tuple-element.18), channel_id=1, source_target_pairs={{0,24},{1,25},{2,26},{3,27},{4,28},{5,29},{6,30},{7,31},{8,0},{9,1... | collective-permute-start | bytes 208904 | tf_op jit(solution)/shard_map/ppermute | solution.py:172
  12.3 4.7 %collective-permute-start.1 = (f32[136,128]{1,0:T(8,128)S(1)}, f32[136,128]{1,0:T(8,128)S(1)}, u32[]{:S(2)}, u32[]{:S(2)}) collective-permute-start(f32[136,128]{1,0:T(8,128)S(1)} %get-tuple-element.18), channel_id=1, source_target_pairs={{0,16},{1,17},{2,18},{3,19},{4,20},{5,21},{6,22},{7,23},{8,24},{9,... | collective-permute-start | bytes 208904 | tf_op jit(solution)/shard_map/ppermute | solution.py:172
  12.7 5.4 %collective-permute-start = (f32[136,128]{1,0:T(8,128)S(1)}, f32[136,128]{1,0:T(8,128)S(1)}, u32[]{:S(2)}, u32[]{:S(2)}) collective-permute-start(f32[136,128]{1,0:T(8,128)S(1)} %get-tuple-element.18), channel_id=1, source_target_pairs={{0,8},{1,9},{2,10},{3,11},{4,12},{5,13},{6,14},{7,15},{8,16},{9,17... | collective-permute-start | bytes 208904 | tf_op jit(solution)/shard_map/ppermute | solution.py:172
  19.0 8.3 %copy-start.1 = (s32[3,16384]{1,0:T(4,128)S(1)}, s32[3,16384]{1,0:T(4,128)}, u32[]{:S(2)}) copy-start(s32[3,16384]{1,0:T(4,128)} %src_coords.3) | copy-start | bytes 589828
  19.0 8.3 %copy-start.6 = (s32[3,8192]{1,0:T(4,128)S(1)}, s32[3,8192]{1,0:T(4,128)}, u32[]{:S(2)}) copy-start(s32[3,8192]{1,0:T(4,128)} %tgt_coords.3) | copy-start | bytes 294916
  19.0 24.7 %all-to-all-start = ((f32[8,136,128]{2,1,0:T(8,128)}), f32[8,136,128]{2,1,0:T(8,128)S(1)}, u32[]{:S(2)}, u32[]{:S(2)}) async-start(f32[8,136,128]{2,1,0:T(8,128)} %broadcast_in_dim.8), calls=%async_computation | async-start | bytes 1114112 | tf_op jit(solution)/shard_map/all_to_all | solution.py:185
  27.3 16.4 %copy-start.2 = (s32[16384]{0:T(1024)S(1)}, s32[16384]{0:T(1024)}, u32[]{:S(2)}) copy-start(s32[16384]{0:T(1024)} %param.10) | copy-start | bytes 196612
  47.1 10.9 %copy-start.4 = (s32[8192]{0:T(1024)S(1)}, s32[8192]{0:T(1024)}, u32[]{:S(2)}) copy-start(s32[8192]{0:T(1024)} %param.11) | copy-start | bytes 98308
  47.2 3.6 %collective-permute-start.3 = (f32[72,128]{1,0:T(8,128)S(1)}, f32[72,128]{1,0:T(8,128)S(1)}, u32[]{:S(2)}, u32[]{:S(2)}) collective-permute-start(f32[72,128]{1,0:T(8,128)S(1)} %get-tuple-element.21), channel_id=1, source_target_pairs={{0,32},{32,0},{64,96},{96,64},{128,160},{160,128},{192,224},{224,1... | collective-permute-start | bytes 110600 | tf_op jit(solution)/shard_map/ppermute | solution.py:189
  50.8 3.7 %collective-permute-start.6 = (f32[72,128]{1,0:T(8,128)S(1)}, f32[72,128]{1,0:T(8,128)S(1)}, u32[]{:S(2)}, u32[]{:S(2)}) collective-permute-start(f32[72,128]{1,0:T(8,128)S(1)} %log_add_fusion.5.m0), channel_id=1, source_target_pairs={{0,192},{32,224},{64,0},{96,32},{128,64},{160,96},{192,128},{224,1... | collective-permute-start | bytes 110600 | tf_op jit(solution)/shard_map/ppermute | solution.py:176
  53.4 4.3 %collective-permute-start.5 = (f32[72,128]{1,0:T(8,128)S(1)}, f32[72,128]{1,0:T(8,128)S(1)}, u32[]{:S(2)}, u32[]{:S(2)}) collective-permute-start(f32[72,128]{1,0:T(8,128)S(1)} %log_add_fusion.5.m0), channel_id=1, source_target_pairs={{0,128},{32,160},{64,192},{96,224},{128,0},{160,32},{192,64},{224,... | collective-permute-start | bytes 110600 | tf_op jit(solution)/shard_map/ppermute | solution.py:176
  53.9 4.2 %collective-permute-start.4 = (f32[72,128]{1,0:T(8,128)S(1)}, f32[72,128]{1,0:T(8,128)S(1)}, u32[]{:S(2)}, u32[]{:S(2)}) collective-permute-start(f32[72,128]{1,0:T(8,128)S(1)} %log_add_fusion.5.m0), channel_id=1, source_target_pairs={{0,64},{32,96},{64,128},{96,160},{128,192},{160,224},{192,0},{224,... | collective-permute-start | bytes 110600 | tf_op jit(solution)/shard_map/ppermute | solution.py:176
  60.9 3.2 %collective-permute-start.9 = (f32[136,128]{1,0:T(8,128)S(1)}, f32[136,128]{1,0:T(8,128)S(1)}, u32[]{:S(2)}, u32[]{:S(2)}) collective-permute-start(f32[136,128]{1,0:T(8,128)S(1)} %get-tuple-element.25), channel_id=1, source_target_pairs={{0,24},{1,25},{2,26},{3,27},{4,28},{5,29},{6,30},{7,31},{8,0},{9,1... | collective-permute-start | bytes 208904 | tf_op jit(solution)/shard_map/ppermute | solution.py:172
  61.3 4.7 %collective-permute-start.8 = (f32[136,128]{1,0:T(8,128)S(1)}, f32[136,128]{1,0:T(8,128)S(1)}, u32[]{:S(2)}, u32[]{:S(2)}) collective-permute-start(f32[136,128]{1,0:T(8,128)S(1)} %get-tuple-element.25), channel_id=1, source_target_pairs={{0,16},{1,17},{2,18},{3,19},{4,20},{5,21},{6,22},{7,23},{8,24},{9,... | collective-permute-start | bytes 208904 | tf_op jit(solution)/shard_map/ppermute | solution.py:172
  62.2 4.4 %collective-permute-start.7 = (f32[136,128]{1,0:T(8,128)S(1)}, f32[136,128]{1,0:T(8,128)S(1)}, u32[]{:S(2)}, u32[]{:S(2)}) collective-permute-start(f32[136,128]{1,0:T(8,128)S(1)} %get-tuple-element.25), channel_id=1, source_target_pairs={{0,8},{1,9},{2,10},{3,11},{4,12},{5,13},{6,14},{7,15},{8,16},{9,17... | collective-permute-start | bytes 208904 | tf_op jit(solution)/shard_map/ppermute | solution.py:172
  86.5 6.2 %collective-permute-start.10 = (f32[72,128]{1,0:T(8,128)S(1)}, f32[72,128]{1,0:T(8,128)S(1)}, u32[]{:S(2)}, u32[]{:S(2)}) collective-permute-start(f32[72,128]{1,0:T(8,128)S(1)} %get-tuple-element.27), channel_id=1, source_target_pairs={{0,32},{32,0},{64,96},{96,64},{128,160},{160,128},{192,224},{224,1... | collective-permute-start | bytes 110600 | tf_op jit(solution)/shard_map/ppermute | solution.py:189
  92.7 2.9 %collective-permute-start.13 = (f32[72,128]{1,0:T(8,128)S(1)}, f32[72,128]{1,0:T(8,128)S(1)}, u32[]{:S(2)}, u32[]{:S(2)}) collective-permute-start(f32[72,128]{1,0:T(8,128)S(1)} %log_add_fusion.4.m0), channel_id=1, source_target_pairs={{0,192},{32,224},{64,0},{96,32},{128,64},{160,96},{192,128},{224,1... | collective-permute-start | bytes 110600 | tf_op jit(solution)/shard_map/ppermute | solution.py:176
  93.3 4.3 %collective-permute-start.12 = (f32[72,128]{1,0:T(8,128)S(1)}, f32[72,128]{1,0:T(8,128)S(1)}, u32[]{:S(2)}, u32[]{:S(2)}) collective-permute-start(f32[72,128]{1,0:T(8,128)S(1)} %log_add_fusion.4.m0), channel_id=1, source_target_pairs={{0,128},{32,160},{64,192},{96,224},{128,0},{160,32},{192,64},{224,... | collective-permute-start | bytes 110600 | tf_op jit(solution)/shard_map/ppermute | solution.py:176
  94.4 4.3 %collective-permute-start.11 = (f32[72,128]{1,0:T(8,128)S(1)}, f32[72,128]{1,0:T(8,128)S(1)}, u32[]{:S(2)}, u32[]{:S(2)}) collective-permute-start(f32[72,128]{1,0:T(8,128)S(1)} %log_add_fusion.4.m0), channel_id=1, source_target_pairs={{0,64},{32,96},{64,128},{96,160},{128,192},{160,224},{192,0},{224,... | collective-permute-start | bytes 110600 | tf_op jit(solution)/shard_map/ppermute | solution.py:176
  101.5 3.5 %collective-permute-start.16 = (f32[136,128]{1,0:T(8,128)S(1)}, f32[136,128]{1,0:T(8,128)S(1)}, u32[]{:S(2)}, u32[]{:S(2)}) collective-permute-start(f32[136,128]{1,0:T(8,128)S(1)} %get-tuple-element.29), channel_id=1, source_target_pairs={{0,24},{1,25},{2,26},{3,27},{4,28},{5,29},{6,30},{7,31},{8,0},{9,1... | collective-permute-start | bytes 208904 | tf_op jit(solution)/shard_map/ppermute | solution.py:172
  103.2 4.7 %collective-permute-start.15 = (f32[136,128]{1,0:T(8,128)S(1)}, f32[136,128]{1,0:T(8,128)S(1)}, u32[]{:S(2)}, u32[]{:S(2)}) collective-permute-start(f32[136,128]{1,0:T(8,128)S(1)} %get-tuple-element.29), channel_id=1, source_target_pairs={{0,16},{1,17},{2,18},{3,19},{4,20},{5,21},{6,22},{7,23},{8,24},{9,... | collective-permute-start | bytes 208904 | tf_op jit(solution)/shard_map/ppermute | solution.py:172
  104.6 4.4 %collective-permute-start.14 = (f32[136,128]{1,0:T(8,128)S(1)}, f32[136,128]{1,0:T(8,128)S(1)}, u32[]{:S(2)}, u32[]{:S(2)}) collective-permute-start(f32[136,128]{1,0:T(8,128)S(1)} %get-tuple-element.29), channel_id=1, source_target_pairs={{0,8},{1,9},{2,10},{3,11},{4,12},{5,13},{6,14},{7,15},{8,16},{9,17... | collective-permute-start | bytes 208904 | tf_op jit(solution)/shard_map/ppermute | solution.py:172
  129.5 5.5 %collective-permute-start.17 = (f32[72,128]{1,0:T(8,128)S(1)}, f32[72,128]{1,0:T(8,128)S(1)}, u32[]{:S(2)}, u32[]{:S(2)}) collective-permute-start(f32[72,128]{1,0:T(8,128)S(1)} %get-tuple-element.33), channel_id=1, source_target_pairs={{0,32},{32,0},{64,96},{96,64},{128,160},{160,128},{192,224},{224,1... | collective-permute-start | bytes 110600 | tf_op jit(solution)/shard_map/ppermute | solution.py:189
  135.0 2.9 %collective-permute-start.20 = (f32[72,128]{1,0:T(8,128)S(1)}, f32[72,128]{1,0:T(8,128)S(1)}, u32[]{:S(2)}, u32[]{:S(2)}) collective-permute-start(f32[72,128]{1,0:T(8,128)S(1)} %log_add_fusion.3), channel_id=1, source_target_pairs={{0,192},{32,224},{64,0},{96,32},{128,64},{160,96},{192,128},{224,1... | collective-permute-start | bytes 110600 | tf_op jit(solution)/shard_map/ppermute | solution.py:176
  136.3 4.3 %collective-permute-start.19 = (f32[72,128]{1,0:T(8,128)S(1)}, f32[72,128]{1,0:T(8,128)S(1)}, u32[]{:S(2)}, u32[]{:S(2)}) collective-permute-start(f32[72,128]{1,0:T(8,128)S(1)} %log_add_fusion.3), channel_id=1, source_target_pairs={{0,128},{32,160},{64,192},{96,224},{128,0},{160,32},{192,64},{224,... | collective-permute-start | bytes 110600 | tf_op jit(solution)/shard_map/ppermute | solution.py:176
  136.8 4.2 %collective-permute-start.18 = (f32[72,128]{1,0:T(8,128)S(1)}, f32[72,128]{1,0:T(8,128)S(1)}, u32[]{:S(2)}, u32[]{:S(2)}) collective-permute-start(f32[72,128]{1,0:T(8,128)S(1)} %log_add_fusion.3), channel_id=1, source_target_pairs={{0,64},{32,96},{64,128},{96,160},{128,192},{160,224},{192,0},{224,... | collective-permute-start | bytes 110600 | tf_op jit(solution)/shard_map/ppermute | solution.py:176
